TPU v7x, 512 devices: a whole 4x8x8 slice. The times are simulated.
512 devices in a mesh: res: 32 (over x, y_hi, core), prog: 16 (over y_lo, z).
Axes of the slice: x: 4, y: 8 (y_hi: 4, y_lo: 2; y = y_hi * 2 + y_lo), z: 8, core: 2. Of those that a mesh axis runs over, the one named last changes fastest.
Arguments:
- queries: bfloat16 [1024, 32768], P('res', 'prog'), may hold values from -14 to 14
- key_vectors: bfloat16 [1024, 32768], P('res', 'prog'), may hold values from -14 to 14
- values: bfloat16 [1024, 32768], P('res', 'prog'), may hold values from -6 to 6
- cotangent: bfloat16 [1024, 32768], P('res', 'prog'), may hold values from -6 to 6
- eligible: int32 [1024, 1024], P('res', 'prog'), may hold values from 0 to 1, as said below
Outputs:
- grad_queries: float32 [1024, 32768], P('res', 'prog')
- grad_keys: float32 [1024, 32768], P('res', 'prog')
- grad_values: float32 [1024, 32768], P('res', 'prog')
Inputs may be any that keep to these rules, and one draw needn't show every extreme that they name: Every resident has at least one eligible program and every program at least one eligible resident.
All inputs are finite; a program needn't handle non-finite values.
Results may differ from a plain program's by a relative error of at most 0.0075.
Values may be sent and summed in bfloat16 or wider, within the bound.
No kernel may reach another device: no remote copies, remote signals or barrier semaphores. Data moves between devices by JAX's collectives and lax.ppermute only.
A program may use at most 64 MiB of HBM per device.

v0:
```python
import math

import jax
import jax.numpy as jnp
from jax import lax
from jax.sharding import PartitionSpec as P

CH = 32


masked_score = -1e30


def shortened(array):
    return jax.tree.map(lambda a: a.astype(jnp.bfloat16) if a.dtype == jnp.float32 else a, array)


def block_grads(query_block, cot_block, key_rows, value_rows, eligible_keys, score_scale):
    scores = jnp.dot(query_block, key_rows.T, preferred_element_type=jnp.float32) * score_scale
    scores = jnp.where(eligible_keys[None, :], scores, masked_score)
    row_max = jnp.max(scores, axis=1, keepdims=True)
    expo = jnp.exp(scores - row_max)
    weights = expo / jnp.sum(expo, axis=1, keepdims=True)
    weights_low = weights.astype(jnp.bfloat16)
    outputs = jnp.dot(weights_low, value_rows, preferred_element_type=jnp.float32)
    weight_grad = jnp.dot(cot_block, value_rows.T, preferred_element_type=jnp.float32)
    delta = jnp.sum(cot_block.astype(jnp.float32) * outputs, axis=1, keepdims=True)
    score_grad = (weights * (weight_grad - delta) * score_scale).astype(jnp.bfloat16)
    query_grad = jnp.dot(score_grad, key_rows, preferred_element_type=jnp.float32)
    dims = (((0,), (0,)), ((), ()))
    key_grad = lax.dot_general(score_grad, query_block, dims, preferred_element_type=jnp.float32)
    value_grad = lax.dot_general(weights_low, cot_block, dims, preferred_element_type=jnp.float32)
    return (query_grad, key_grad, value_grad)


def pass_grads(queries, key_cube, value_cube, cot_cube, eligible_keys, item_axis):
    item_count = queries.shape[item_axis]
    length = queries.shape[1 - item_axis]
    channels = queries.shape[2]
    block_rows = min(512, length)
    block_count = length // block_rows
    score_scale = 1.0 / math.sqrt(channels)
    offsets = jnp.arange(block_count, dtype=jnp.int32) * block_rows

    def item_body(item_index, running):
        out_queries, out_keys, out_values = running
        query_item = lax.dynamic_index_in_dim(queries, item_index, item_axis, keepdims=False)
        key_item = lax.dynamic_index_in_dim(key_cube, item_index, item_axis, keepdims=False)
        value_item = lax.dynamic_index_in_dim(value_cube, item_index, item_axis, keepdims=False)
        cot_item = lax.dynamic_index_in_dim(cot_cube, item_index, item_axis, keepdims=False)
        keep_item = lax.dynamic_index_in_dim(eligible_keys, item_index, item_axis, keepdims=False)

        def block_step(partial_value, offset):
            key_sum, value_sum = partial_value
            query_block = lax.dynamic_slice_in_dim(query_item, offset, block_rows, 0)
            cot_block = lax.dynamic_slice_in_dim(cot_item, offset, block_rows, 0)
            query_grad, key_grad, value_grad = block_grads(
                query_block, cot_block, key_item, value_item, keep_item, score_scale
            )
            return ((key_sum + key_grad, value_sum + value_grad), query_grad.astype(jnp.bfloat16))

        zero_sums = (
            jnp.zeros((length, channels), jnp.float32),
            jnp.zeros((length, channels), jnp.float32),
        )
        (key_sum, value_sum), query_blocks = lax.scan(block_step, zero_sums, offsets)
        query_total = query_blocks.reshape(length, channels)
        out_queries = lax.dynamic_update_index_in_dim(
            out_queries, query_total, item_index, item_axis
        )
        out_keys = lax.dynamic_update_index_in_dim(
            out_keys, key_sum.astype(jnp.bfloat16), item_index, item_axis
        )
        out_values = lax.dynamic_update_index_in_dim(
            out_values, value_sum.astype(jnp.bfloat16), item_index, item_axis
        )
        return (out_queries, out_keys, out_values)

    empty = jnp.zeros(queries.shape, jnp.bfloat16)
    return lax.fori_loop(0, item_count, item_body, (empty, empty, empty))


def regroup_rows(bundle):
    return jax.tree.map(
        lambda part, own: part.astype(own.dtype),
        lax.all_to_all(shortened(bundle), "prog", split_axis=0, concat_axis=1, tiled=True),
        bundle,
    )


def side_grads(gathered, item_axis):
    query_part, key_part, value_part, cot_part, plane_part = gathered
    return pass_grads(query_part, key_part, value_part, cot_part, plane_part > 0.5, item_axis)


def per_device(queries, key_vectors, values, cotangent, eligible):
    rows_dev, width = queries.shape
    channels = CH
    progs_dev = width // channels
    shape_cube = (rows_dev, progs_dev, channels)
    plane = eligible.astype(jnp.bfloat16)
    bundle = (
        queries.reshape(shape_cube),
        key_vectors.reshape(shape_cube),
        values.reshape(shape_cube),
        cotangent.reshape(shape_cube),
        plane,
    )
    row_inputs = regroup_rows(bundle)
    row_local = side_grads(row_inputs, 0)
    row_grads = (
        lax.all_to_all(row_local[0], "prog", split_axis=1, concat_axis=0, tiled=True),
        lax.all_to_all(row_local[1], "prog", split_axis=1, concat_axis=0, tiled=True),
        lax.all_to_all(row_local[2], "prog", split_axis=1, concat_axis=0, tiled=True),
    )
    col_inputs = (
        lax.all_to_all(bundle[0], "res", split_axis=1, concat_axis=0, tiled=True),
        lax.all_to_all(bundle[1], "res", split_axis=1, concat_axis=0, tiled=True),
        lax.all_to_all(bundle[2], "res", split_axis=1, concat_axis=0, tiled=True),
        lax.all_to_all(bundle[3], "res", split_axis=1, concat_axis=0, tiled=True),
        lax.all_to_all(bundle[4], "res", split_axis=1, concat_axis=0, tiled=True),
    )
    col_local = side_grads(col_inputs, 1)
    col_grads = (
        lax.all_to_all(col_local[0], "res", split_axis=0, concat_axis=1, tiled=True),
        lax.all_to_all(col_local[1], "res", split_axis=0, concat_axis=1, tiled=True),
        lax.all_to_all(col_local[2], "res", split_axis=0, concat_axis=1, tiled=True),
    )
    totals = [
        (row_grads[slot].astype(jnp.float32) + col_grads[slot].astype(jnp.float32)).reshape(
            rows_dev, width
        )
        for slot in range(3)
    ]
    return (totals[0], totals[1], totals[2])


def solution(mesh):
    in_specs = (
        P("res", "prog"),
        P("res", "prog"),
        P("res", "prog"),
        P("res", "prog"),
        P("res", "prog"),
    )
    out_specs = (P("res", "prog"), P("res", "prog"), P("res", "prog"))
    return jax.shard_map(
        per_device, mesh=mesh, in_specs=in_specs, out_specs=out_specs, check_vma=False
    )
```

profile of v0, /device:TPU:1, one launch (start us, length us, event | category | flops | bytes accessed | tf_op | source)
XLA Modules:
  0.0 286.8 jit_solution(4173276952181604868)
XLA Ops:
  2.0 12.0 %all-to-all-start.3 = ((bf16[16,2,64]{2,1,0:T(2,128)(2,1)}), bf16[16,2,64]{2,1,0:T(2,128)(2,1)S(1)}, u32[]{:S(2)}, u32[]{:S(2)}) async-start(bf16[16,2,64]{2,1,0:T(2,128)(2,1)} %bitcast.8), calls=%async_computation.3 | async-start | bytes 16384 | tf_op jit(solution)/shard_map/all_to_all | solution.py:86
  15.4 5.8 %all-to-all-done.3 = bf16[16,2,64]{2,1,0:T(2,128)(2,1)S(1)} async-done(((bf16[16,2,64]{2,1,0:T(2,128)(2,1)}), bf16[16,2,64]{2,1,0:T(2,128)(2,1)S(1)}, u32[]{:S(2)}, u32[]{:S(2)}) %all-to-all-start.3) | async-done | bytes 4128 | tf_op jit(solution)/shard_map/all_to_all | solution.py:86
  21.2 10.9 %all-to-all-start.9 = ((bf16[32,32,2]{0,2,1:T(2,128)(2,1)}), bf16[32,32,2]{0,2,1:T(2,128)(2,1)S(1)}, u32[]{:S(2)}, u32[]{:S(2)}) async-start(bf16[32,32,2]{0,2,1:T(2,128)(2,1)} %bitcast.23), calls=%async_computation.9 | async-start | bytes 32768 | tf_op jit(solution)/shard_map/all_to_all | solution.py:121
  34.6 6.8 %all-to-all-done.9 = bf16[32,32,2]{0,2,1:T(2,128)(2,1)S(1)} async-done(((bf16[32,32,2]{0,2,1:T(2,128)(2,1)}), bf16[32,32,2]{0,2,1:T(2,128)(2,1)S(1)}, u32[]{:S(2)}, u32[]{:S(2)}) %all-to-all-start.9) | async-done | bytes 4128 | tf_op jit(solution)/shard_map/all_to_all | solution.py:121
  47.1 5.9 %all-to-all-done = bf16[16,2,2048]{2,1,0:T(2,128)(2,1)S(1)} async-done(((bf16[16,2,2048]{2,1,0:T(2,128)(2,1)}), bf16[16,2,2048]{2,1,0:T(2,128)(2,1)S(1)}, u32[]{:S(2)}, u32[]{:S(2)}) %all-to-all-start) | async-done | bytes 131104 | tf_op jit(solution)/shard_map/all_to_all | solution.py:86
  53.1 4.3 %all-to-all-start.2 = ((bf16[16,2,2048]{2,1,0:T(2,128)(2,1)}), bf16[16,2,2048]{2,1,0:T(2,128)(2,1)S(1)}, u32[]{:S(2)}, u32[]{:S(2)}) async-start(bf16[16,2,2048]{2,1,0:T(2,128)(2,1)} %reshape.99), calls=%async_computation.2 | async-start | bytes 262144 | tf_op jit(solution)/shard_map/all_to_all | solution.py:86
  58.8 5.9 %all-to-all-done.2 = bf16[16,2,2048]{2,1,0:T(2,128)(2,1)S(1)} async-done(((bf16[16,2,2048]{2,1,0:T(2,128)(2,1)}), bf16[16,2,2048]{2,1,0:T(2,128)(2,1)S(1)}, u32[]{:S(2)}, u32[]{:S(2)}) %all-to-all-start.2) | async-done | bytes 131104 | tf_op jit(solution)/shard_map/all_to_all | solution.py:86
  64.8 4.0 %all-to-all-start.4 = ((bf16[16,2,2048]{2,1,0:T(2,128)(2,1)}), bf16[16,2,2048]{2,1,0:T(2,128)(2,1)S(1)}, u32[]{:S(2)}, u32[]{:S(2)}) async-start(bf16[16,2,2048]{2,1,0:T(2,128)(2,1)} %reshape.101), calls=%async_computation.4 | async-start | bytes 262144 | tf_op jit(solution)/shard_map/all_to_all | solution.py:86
  70.3 6.0 %all-to-all-done.4 = bf16[16,2,2048]{2,1,0:T(2,128)(2,1)S(1)} async-done(((bf16[16,2,2048]{2,1,0:T(2,128)(2,1)}), bf16[16,2,2048]{2,1,0:T(2,128)(2,1)S(1)}, u32[]{:S(2)}, u32[]{:S(2)}) %all-to-all-start.4) | async-done | bytes 131104 | tf_op jit(solution)/shard_map/all_to_all | solution.py:86
  81.3 5.8 %all-to-all-done.1 = bf16[16,2,2048]{2,1,0:T(2,128)(2,1)S(1)} async-done(((bf16[16,2,2048]{2,1,0:T(2,128)(2,1)}), bf16[16,2,2048]{2,1,0:T(2,128)(2,1)S(1)}, u32[]{:S(2)}, u32[]{:S(2)}) %all-to-all-start.1) | async-done | bytes 131104 | tf_op jit(solution)/shard_map/all_to_all | solution.py:86
  87.2 7.4 %all-to-all-start.6 = ((bf16[32,2,1024]{2,1,0:T(2,128)(2,1)}), bf16[32,2,1024]{2,1,0:T(2,128)(2,1)S(1)}, u32[]{:S(2)}, u32[]{:S(2)}) async-start(bf16[32,2,1024]{2,1,0:T(2,128)(2,1)} %reshape.105), calls=%async_computation.6 | async-start | bytes 262144 | tf_op jit(solution)/shard_map/all_to_all | solution.py:117
  96.1 9.5 %all-to-all-done.6 = bf16[32,2,1024]{2,1,0:T(2,128)(2,1)S(1)} async-done(((bf16[32,2,1024]{2,1,0:T(2,128)(2,1)}), bf16[32,2,1024]{2,1,0:T(2,128)(2,1)S(1)}, u32[]{:S(2)}, u32[]{:S(2)}) %all-to-all-start.6) | async-done | bytes 131104 | tf_op jit(solution)/shard_map/all_to_all | solution.py:117
  105.6 3.6 %all-to-all-start.8 = ((bf16[32,2,1024]{2,1,0:T(2,128)(2,1)}), bf16[32,2,1024]{2,1,0:T(2,128)(2,1)S(1)}, u32[]{:S(2)}, u32[]{:S(2)}) async-start(bf16[32,2,1024]{2,1,0:T(2,128)(2,1)} %reshape.109), calls=%async_computation.8 | async-start | bytes 262144 | tf_op jit(solution)/shard_map/all_to_all | solution.py:118
  110.8 9.3 %all-to-all-done.8 = bf16[32,2,1024]{2,1,0:T(2,128)(2,1)S(1)} async-done(((bf16[32,2,1024]{2,1,0:T(2,128)(2,1)}), bf16[32,2,1024]{2,1,0:T(2,128)(2,1)S(1)}, u32[]{:S(2)}, u32[]{:S(2)}) %all-to-all-start.8) | async-done | bytes 131104 | tf_op jit(solution)/shard_map/all_to_all | solution.py:118
  120.1 3.6 %all-to-all-start.10 = ((bf16[32,2,1024]{2,1,0:T(2,128)(2,1)}), bf16[32,2,1024]{2,1,0:T(2,128)(2,1)S(1)}, u32[]{:S(2)}, u32[]{:S(2)}) async-start(bf16[32,2,1024]{2,1,0:T(2,128)(2,1)} %reshape.111), calls=%async_computation.10 | async-start | bytes 262144 | tf_op jit(solution)/shard_map/all_to_all | solution.py:119
  127.6 7.0 %all-to-all-done.10 = bf16[32,2,1024]{2,1,0:T(2,128)(2,1)S(1)} async-done(((bf16[32,2,1024]{2,1,0:T(2,128)(2,1)}), bf16[32,2,1024]{2,1,0:T(2,128)(2,1)S(1)}, u32[]{:S(2)}, u32[]{:S(2)}) %all-to-all-start.10) | async-done | bytes 131104 | tf_op jit(solution)/shard_map/all_to_all | solution.py:119
  134.6 3.8 %all-to-all-start.7 = ((bf16[32,2,1024]{2,1,0:T(2,128)(2,1)}), bf16[32,2,1024]{2,1,0:T(2,128)(2,1)S(1)}, u32[]{:S(2)}, u32[]{:S(2)}) async-start(bf16[32,2,1024]{2,1,0:T(2,128)(2,1)} %reshape.107), calls=%async_computation.7 | async-start | bytes 262144 | tf_op jit(solution)/shard_map/all_to_all | solution.py:120
  138.4 29.5 %while.109 = (s32[]{:T(128)}, bf16[2,1024,32]{2,1,0:T(8,128)(2,1)}, bf16[2,1024,32]{1,2,0:T(8,128)(2,1)}, bf16[2,1024,32]{1,2,0:T(8,128)(2,1)}, bf16[2,1024,32]{...) while((s32[]{:T(128)}, bf16[2,1024,32]{2,1,0:T(8,128)(2,1)}, ...), condition=%wide.region_6.7_spmd.clone, body=%wide.region_0.6_spmd.clone.sunk | while | flops 210500096 | bytes 22040108 | solution.py:80
  138.6 13.0 %while.112 = (s32[]{:T(128)}, f32[1024,32]{0,1:T(8,128)S(1)}, f32[1024,32]{0,1:T(8,128)S(1)}, bf16[2,512,32]{1,2,0:T(8,128)(2,1)S(1)}, pred[1024]{0:T(1024)(128)...) while((s32[]{:T(128)}, f32[1024,32]{0,1:T(8,128)S(1)}, ...), condition=%wide.region_5.5_spmd.clone, body=%wide.region_1.4_spmd.clone.sunk | while | flops 210434560 | bytes 19612884 | solution.py:66
  153.4 13.0 %while.112 = (s32[]{:T(128)}, f32[1024,32]{0,1:T(8,128)S(1)}, f32[1024,32]{0,1:T(8,128)S(1)}, bf16[2,512,32]{1,2,0:T(8,128)(2,1)S(1)}, pred[1024]{0:T(1024)(128)...) while((s32[]{:T(128)}, f32[1024,32]{0,1:T(8,128)S(1)}, ...), condition=%wide.region_5.5_spmd.clone, body=%wide.region_1.4_spmd.clone.sunk | while | flops 210434560 | bytes 19612884 | solution.py:66
  177.4 4.6 %all-to-all-done.14 = bf16[16,2,2048]{2,1,0:T(2,128)(2,1)S(1)} async-done(((bf16[16,2,2048]{2,1,0:T(2,128)(2,1)}), bf16[16,2,2048]{2,1,0:T(2,128)(2,1)S(1)}, u32[]{:S(2)}, u32[]{:S(2)}) %all-to-all-start.14) | async-done | bytes 131104 | tf_op jit(solution)/shard_map/all_to_all | solution.py:114
  182.0 4.5 %all-to-all-start.5 = ((bf16[16,2,2048]{2,1,0:T(2,128)(2,1)}), bf16[16,2,2048]{2,1,0:T(2,128)(2,1)S(1)}, u32[]{:S(2)}, u32[]{:S(2)}) async-start(bf16[16,2,2048]{2,1,0:T(2,128)(2,1)} %reshape.103), calls=%async_computation.5 | async-start | bytes 262144 | tf_op jit(solution)/shard_map/all_to_all | solution.py:112
  194.0 4.6 %all-to-all-start.12 = ((bf16[16,2,2048]{2,1,0:T(2,128)(2,1)}), bf16[16,2,2048]{2,1,0:T(2,128)(2,1)S(1)}, u32[]{:S(2)}, u32[]{:S(2)}) async-start(bf16[16,2,2048]{2,1,0:T(2,128)(2,1)} %reshape.115), calls=%async_computation.12 | async-start | bytes 262144 | tf_op jit(solution)/shard_map/all_to_all | solution.py:113
  198.7 28.8 %while.111 = (s32[]{:T(128)}, bf16[1024,2,32]{0,2,1:T(8,128)(2,1)}, bf16[1024,2,32]{0,2,1:T(8,128)(2,1)S(1)}, bf16[1024,2,32]{0,2,1:T(8,128)(2,1)S(1)}, bf16[102...) while((s32[]{:T(128)}, bf16[1024,2,32]{0,2,1:T(8,128)(2,1)}, ...), condition=%wide.region_13.14_spmd.clone, body=%wide.region_7.13_spmd.clone.sunk | while | flops 210500096 | bytes 20925940 | solution.py:80
  198.9 13.4 %while.113 = (s32[]{:T(128)}, f32[1024,32]{0,1:T(8,128)S(1)}, f32[1024,32]{0,1:T(8,128)S(1)}, bf16[2,512,32]{1,2,0:T(8,128)(2,1)S(1)}, pred[1024]{0:T(1024)(128)...) while((s32[]{:T(128)}, f32[1024,32]{0,1:T(8,128)S(1)}, ...), condition=%wide.region_12.12_spmd.clone, body=%wide.region_8.11_spmd.clone.sunk | while | flops 210434560 | bytes 19612884 | solution.py:66
  213.3 13.4 %while.113 = (s32[]{:T(128)}, f32[1024,32]{0,1:T(8,128)S(1)}, f32[1024,32]{0,1:T(8,128)S(1)}, bf16[2,512,32]{1,2,0:T(8,128)(2,1)S(1)}, pred[1024]{0:T(1024)(128)...) while((s32[]{:T(128)}, f32[1024,32]{0,1:T(8,128)S(1)}, ...), condition=%wide.region_12.12_spmd.clone, body=%wide.region_8.11_spmd.clone.sunk | while | flops 210434560 | bytes 19612884 | solution.py:66
  229.1 10.8 %all-to-all-start.15 = ((bf16[32,2,1024]{2,1,0:T(2,128)(2,1)}), bf16[32,2,1024]{2,1,0:T(2,128)(2,1)S(1)}, u32[]{:S(2)}, u32[]{:S(2)}) async-start(bf16[32,2,1024]{2,1,0:T(2,128)(2,1)} %reshape.121), calls=%async_computation.15 | async-start | bytes 262144 | tf_op jit(solution)/shard_map/all_to_all | solution.py:127
  246.5 4.7 %all-to-all-done.15 = bf16[32,2,1024]{2,1,0:T(2,128)(2,1)S(1)} async-done(((bf16[32,2,1024]{2,1,0:T(2,128)(2,1)}), bf16[32,2,1024]{2,1,0:T(2,128)(2,1)S(1)}, u32[]{:S(2)}, u32[]{:S(2)}) %all-to-all-start.15) | async-done | bytes 131104 | tf_op jit(solution)/shard_map/all_to_all | solution.py:127
  251.2 5.1 %all-to-all-start.11 = ((bf16[32,2,1024]{2,1,0:T(2,128)(2,1)}), bf16[32,2,1024]{2,1,0:T(2,128)(2,1)S(1)}, u32[]{:S(2)}, u32[]{:S(2)}) async-start(bf16[32,2,1024]{2,1,0:T(2,128)(2,1)} %reshape.113), calls=%async_computation.11 | async-start | bytes 262144 | tf_op jit(solution)/shard_map/all_to_all | solution.py:125
  258.5 9.1 %all-to-all-done.11 = bf16[32,2,1024]{2,1,0:T(2,128)(2,1)S(1)} async-done(((bf16[32,2,1024]{2,1,0:T(2,128)(2,1)}), bf16[32,2,1024]{2,1,0:T(2,128)(2,1)S(1)}, u32[]{:S(2)}, u32[]{:S(2)}) %all-to-all-start.11) | async-done | bytes 131104 | tf_op jit(solution)/shard_map/all_to_all | solution.py:125
  267.6 3.9 %all-to-all-start.13 = ((bf16[32,2,1024]{2,1,0:T(2,128)(2,1)}), bf16[32,2,1024]{2,1,0:T(2,128)(2,1)S(1)}, u32[]{:S(2)}, u32[]{:S(2)}) async-start(bf16[32,2,1024]{2,1,0:T(2,128)(2,1)} %reshape.117), calls=%async_computation.13 | async-start | bytes 262144 | tf_op jit(solution)/shard_map/all_to_all | solution.py:126
  273.7 8.7 %all-to-all-done.13 = bf16[32,2,1024]{2,1,0:T(2,128)(2,1)S(1)} async-done(((bf16[32,2,1024]{2,1,0:T(2,128)(2,1)}), bf16[32,2,1024]{2,1,0:T(2,128)(2,1)S(1)}, u32[]{:S(2)}, u32[]{:S(2)}) %all-to-all-start.13) | async-done | bytes 131104 | tf_op jit(solution)/shard_map/all_to_all | solution.py:126
  (241 shorter events, 100.9 us)
Async XLA Ops:
  0.6 45.0 %copy-start.2 = (bf16[32,2048]{1,0:T(8,128)(2,1)S(1)}, bf16[32,2048]{1,0:T(8,128)(2,1)}, u32[]{:S(2)}) copy-start(bf16[32,2048]{1,0:T(8,128)(2,1)} %param.14) | copy-start | bytes 393220
  2.0 19.2 %all-to-all-start.3 = ((bf16[16,2,64]{2,1,0:T(2,128)(2,1)}), bf16[16,2,64]{2,1,0:T(2,128)(2,1)S(1)}, u32[]{:S(2)}, u32[]{:S(2)}) async-start(bf16[16,2,64]{2,1,0:T(2,128)(2,1)} %bitcast.8), calls=%async_computation.3 | async-start | bytes 16384 | tf_op jit(solution)/shard_map/all_to_all | solution.py:86
  21.2 20.2 %all-to-all-start.9 = ((bf16[32,32,2]{0,2,1:T(2,128)(2,1)}), bf16[32,32,2]{0,2,1:T(2,128)(2,1)S(1)}, u32[]{:S(2)}, u32[]{:S(2)}) async-start(bf16[32,32,2]{0,2,1:T(2,128)(2,1)} %bitcast.23), calls=%async_computation.9 | async-start | bytes 32768 | tf_op jit(solution)/shard_map/all_to_all | solution.py:121
  32.2 25.2 %copy-start.3 = (bf16[32,2048]{1,0:T(8,128)(2,1)S(1)}, bf16[32,2048]{1,0:T(8,128)(2,1)}, u32[]{:S(2)}) copy-start(bf16[32,2048]{1,0:T(8,128)(2,1)} %param.15) | copy-start | bytes 393220
  41.5 0.6 copy-start.10
  42.1 11.0 %all-to-all-start = ((bf16[16,2,2048]{2,1,0:T(2,128)(2,1)}), bf16[16,2,2048]{2,1,0:T(2,128)(2,1)S(1)}, u32[]{:S(2)}, u32[]{:S(2)}) async-start(bf16[16,2,2048]{2,1,0:T(2,128)(2,1)} %reshape.95), calls=%async_computation | async-start | bytes 262144 | tf_op jit(solution)/shard_map/all_to_all | solution.py:86
  45.6 23.2 %copy-start.4 = (bf16[32,2048]{1,0:T(8,128)(2,1)S(1)}, bf16[32,2048]{1,0:T(8,128)(2,1)}, u32[]{:S(2)}) copy-start(bf16[32,2048]{1,0:T(8,128)(2,1)} %param.16) | copy-start | bytes 393220
  53.1 11.7 %all-to-all-start.2 = ((bf16[16,2,2048]{2,1,0:T(2,128)(2,1)}), bf16[16,2,2048]{2,1,0:T(2,128)(2,1)S(1)}, u32[]{:S(2)}, u32[]{:S(2)}) async-start(bf16[16,2,2048]{2,1,0:T(2,128)(2,1)} %reshape.99), calls=%async_computation.2 | async-start | bytes 262144 | tf_op jit(solution)/shard_map/all_to_all | solution.py:86
  64.8 11.5 %all-to-all-start.4 = ((bf16[16,2,2048]{2,1,0:T(2,128)(2,1)}), bf16[16,2,2048]{2,1,0:T(2,128)(2,1)S(1)}, u32[]{:S(2)}, u32[]{:S(2)}) async-start(bf16[16,2,2048]{2,1,0:T(2,128)(2,1)} %reshape.101), calls=%async_computation.4 | async-start | bytes 262144 | tf_op jit(solution)/shard_map/all_to_all | solution.py:86
  76.3 10.9 %all-to-all-start.1 = ((bf16[16,2,2048]{2,1,0:T(2,128)(2,1)}), bf16[16,2,2048]{2,1,0:T(2,128)(2,1)S(1)}, u32[]{:S(2)}, u32[]{:S(2)}) async-start(bf16[16,2,2048]{2,1,0:T(2,128)(2,1)} %reshape.97), calls=%async_computation.1 | async-start | bytes 262144 | tf_op jit(solution)/shard_map/all_to_all | solution.py:86
  87.2 18.4 %all-to-all-start.6 = ((bf16[32,2,1024]{2,1,0:T(2,128)(2,1)}), bf16[32,2,1024]{2,1,0:T(2,128)(2,1)S(1)}, u32[]{:S(2)}, u32[]{:S(2)}) async-start(bf16[32,2,1024]{2,1,0:T(2,128)(2,1)} %reshape.105), calls=%async_computation.6 | async-start | bytes 262144 | tf_op jit(solution)/shard_map/all_to_all | solution.py:117
  105.6 14.5 %all-to-all-start.8 = ((bf16[32,2,1024]{2,1,0:T(2,128)(2,1)}), bf16[32,2,1024]{2,1,0:T(2,128)(2,1)S(1)}, u32[]{:S(2)}, u32[]{:S(2)}) async-start(bf16[32,2,1024]{2,1,0:T(2,128)(2,1)} %reshape.109), calls=%async_computation.8 | async-start | bytes 262144 | tf_op jit(solution)/shard_map/all_to_all | solution.py:118
  120.1 14.5 %all-to-all-start.10 = ((bf16[32,2,1024]{2,1,0:T(2,128)(2,1)}), bf16[32,2,1024]{2,1,0:T(2,128)(2,1)S(1)}, u32[]{:S(2)}, u32[]{:S(2)}) async-start(bf16[32,2,1024]{2,1,0:T(2,128)(2,1)} %reshape.111), calls=%async_computation.10 | async-start | bytes 262144 | tf_op jit(solution)/shard_map/all_to_all | solution.py:119
  134.6 35.8 %all-to-all-start.7 = ((bf16[32,2,1024]{2,1,0:T(2,128)(2,1)}), bf16[32,2,1024]{2,1,0:T(2,128)(2,1)S(1)}, u32[]{:S(2)}, u32[]{:S(2)}) async-start(bf16[32,2,1024]{2,1,0:T(2,128)(2,1)} %reshape.107), calls=%async_computation.7 | async-start | bytes 262144 | tf_op jit(solution)/shard_map/all_to_all | solution.py:120
  138.6 13.7 %copy-start.7 = (bf16[2,1024,32]{1,2,0:T(8,128)(2,1)S(1)}, bf16[2,1024,32]{1,2,0:T(8,128)(2,1)}, u32[]{:S(2)}) copy-start(bf16[2,1024,32]{1,2,0:T(8,128)(2,1)} %get-tuple-element.1153) | copy-start | bytes 393220 | tf_op jit(solution)/shard_map/while
  152.3 0.9 copy-start.8
  153.4 13.7 %copy-start.7 = (bf16[2,1024,32]{1,2,0:T(8,128)(2,1)S(1)}, bf16[2,1024,32]{1,2,0:T(8,128)(2,1)}, u32[]{:S(2)}) copy-start(bf16[2,1024,32]{1,2,0:T(8,128)(2,1)} %get-tuple-element.1153) | copy-start | bytes 393220 | tf_op jit(solution)/shard_map/while
  167.1 0.9 copy-start.8
  168.0 18.6 %copy-start.11 = (bf16[32,32,2]{0,2,1:T(2,128)(2,1)S(1)}, bf16[32,32,2]{0,2,1:T(2,128)(2,1)}, u32[]{:S(2)}) copy-start(bf16[32,32,2]{0,2,1:T(2,128)(2,1)} %copy-done.10) | copy-start | bytes 12292
  168.0 18.7 %copy-start.9 = (bf16[2,1024,32]{1,2,0:T(8,128)(2,1)S(1)}, bf16[2,1024,32]{1,2,0:T(8,128)(2,1)}, u32[]{:S(2)}) copy-start(bf16[2,1024,32]{1,2,0:T(8,128)(2,1)} %get-tuple-element.455) | copy-start | bytes 393220
  170.4 0.7 copy-start
  171.1 10.9 %all-to-all-start.14 = ((bf16[16,2,2048]{2,1,0:T(2,128)(2,1)}), bf16[16,2,2048]{2,1,0:T(2,128)(2,1)S(1)}, u32[]{:S(2)}, u32[]{:S(2)}) async-start(bf16[16,2,2048]{2,1,0:T(2,128)(2,1)} %reshape.119), calls=%async_computation.14 | async-start | bytes 262144 | tf_op jit(solution)/shard_map/all_to_all | solution.py:114
  182.0 12.0 %all-to-all-start.5 = ((bf16[16,2,2048]{2,1,0:T(2,128)(2,1)}), bf16[16,2,2048]{2,1,0:T(2,128)(2,1)S(1)}, u32[]{:S(2)}, u32[]{:S(2)}) async-start(bf16[16,2,2048]{2,1,0:T(2,128)(2,1)} %reshape.103), calls=%async_computation.5 | async-start | bytes 262144 | tf_op jit(solution)/shard_map/all_to_all | solution.py:112
  188.6 0.9 copy-start.1
  188.9 9.7 %copy-start.5 = (bf16[1024,2,32]{0,2,1:T(8,128)(2,1)S(1)}, bf16[1024,2,32]{0,2,1:T(8,128)(2,1)}, u32[]{:S(2)}) copy-start(bf16[1024,2,32]{0,2,1:T(8,128)(2,1)} %custom-call.15) | copy-start | bytes 393220
  189.2 9.5 %copy-start.6 = (bf16[1024,2,32]{0,2,1:T(8,128)(2,1)S(1)}, bf16[1024,2,32]{0,2,1:T(8,128)(2,1)}, u32[]{:S(2)}) copy-start(bf16[1024,2,32]{0,2,1:T(8,128)(2,1)} %custom-call.14) | copy-start | bytes 393220
  194.0 35.0 %all-to-all-start.12 = ((bf16[16,2,2048]{2,1,0:T(2,128)(2,1)}), bf16[16,2,2048]{2,1,0:T(2,128)(2,1)S(1)}, u32[]{:S(2)}, u32[]{:S(2)}) async-start(bf16[16,2,2048]{2,1,0:T(2,128)(2,1)} %reshape.115), calls=%async_computation.12 | async-start | bytes 262144 | tf_op jit(solution)/shard_map/all_to_all | solution.py:113
  229.1 22.1 %all-to-all-start.15 = ((bf16[32,2,1024]{2,1,0:T(2,128)(2,1)}), bf16[32,2,1024]{2,1,0:T(2,128)(2,1)S(1)}, u32[]{:S(2)}, u32[]{:S(2)}) async-start(bf16[32,2,1024]{2,1,0:T(2,128)(2,1)} %reshape.121), calls=%async_computation.15 | async-start | bytes 262144 | tf_op jit(solution)/shard_map/all_to_all | solution.py:127
  251.2 16.4 %all-to-all-start.11 = ((bf16[32,2,1024]{2,1,0:T(2,128)(2,1)}), bf16[32,2,1024]{2,1,0:T(2,128)(2,1)S(1)}, u32[]{:S(2)}, u32[]{:S(2)}) async-start(bf16[32,2,1024]{2,1,0:T(2,128)(2,1)} %reshape.113), calls=%async_computation.11 | async-start | bytes 262144 | tf_op jit(solution)/shard_map/all_to_all | solution.py:125
  267.6 14.8 %all-to-all-start.13 = ((bf16[32,2,1024]{2,1,0:T(2,128)(2,1)}), bf16[32,2,1024]{2,1,0:T(2,128)(2,1)S(1)}, u32[]{:S(2)}, u32[]{:S(2)}) async-start(bf16[32,2,1024]{2,1,0:T(2,128)(2,1)} %reshape.117), calls=%async_computation.13 | async-start | bytes 262144 | tf_op jit(solution)/shard_map/all_to_all | solution.py:126
where the time goes:
time: 288 us; the launch traced here: 287 us
  waiting for transfers between devices  92.3 us (32%)
  starting transfers between devices  89.1 us (31%)
  local copies, waits for them, and re-layouts  49.3 us (17%)
  matrix products  22.7 us (8%)
  loops' own time  16.7 us (6%)
  other arithmetic  15.4 us (5%)
    all_to_all x5, waiting for transfers between devices, regroup_rows(): lax.all_to_all(shortened(bundle), 'prog', split_axis=0, concat_axis=1, ti...  29.5 us
    all_to_all x5, starting transfers between devices, regroup_rows(): lax.all_to_all(shortened(bundle), 'prog', split_axis=0, concat_axis=1, ti...  27.2 us
    unnamed x54, local copies, waits for them, and re-layouts  21.4 us
    another operation x4, loops' own time, item_body(): lax.scan(block_step, zero_sums, offsets)  16.3 us
    all_to_all x1, starting transfers between devices, per_device(): lax.all_to_all(bundle[4], 'res', split_axis=1, concat_axis=0, tiled=True)  10.9 us
    all_to_all x1, starting transfers between devices, per_device(): lax.all_to_all(col_local[2], 'res', split_axis=0, concat_axis=1, tiled=True)  10.8 us
    all_to_all x1, waiting for transfers between devices, per_device(): lax.all_to_all(bundle[0], 'res', split_axis=1, concat_axis=0, tiled=True)  9.55 us
    all_to_all x1, waiting for transfers between devices, per_device(): lax.all_to_all(bundle[1], 'res', split_axis=1, concat_axis=0, tiled=True)  9.31 us
  transfers between devices with their start and end apart: 16, of which 14 were waited for; matrix products, arithmetic and copies ran while one was open for 28% of the time, Pallas kernels for 0%

commit v1 on v0

v1 whole, which is shorter than its diff:
```python
import functools
import math

import jax
import jax.numpy as jnp
from jax import lax
from jax.experimental import pallas as pl
from jax.experimental.pallas import tpu as pltpu
from jax.sharding import PartitionSpec as P

CH = 32
LANES = 128
BLOCKS = LANES // CH
SCALE = 1.0 / math.sqrt(CH)
EXP2_SCALE = SCALE * math.log2(math.e)
masked_score = -1e30
INTERPRET = False
QB = 256
KEYS = 1024
KC = 256

f32 = jnp.float32
bf16 = jnp.bfloat16


def iota(shape, dim):
    return lax.broadcasted_iota(jnp.int32, shape, dim)


def dot(x, y, cx=1, cy=0):
    return lax.dot_general(x, y, (((cx,), (cy,)), ((), ())), preferred_element_type=f32)


def call(body, outs, scratch, *args):
    return pl.pallas_call(
        body,
        out_shape=outs,
        in_specs=[pl.BlockSpec(memory_space=pltpu.VMEM)] * len(args),
        out_specs=jax.tree.map(lambda _: pl.BlockSpec(memory_space=pltpu.VMEM), outs),
        scratch_shapes=scratch,
        interpret=INTERPRET,
        compiler_params=pltpu.CompilerParams(vmem_limit_bytes=48 * 2**20),
    )(*args)


def pack_rows_body(q_ref, k_ref, v_ref, g_ref, e_ref, out_ref, scr_ref):
    for t, ref in enumerate((q_ref, k_ref, v_ref, g_ref)):
        for l in range(16):
            scr_ref[t, pl.ds(l, 32, stride=16), :] = ref[:, l * LANES : (l + 1) * LANES].astype(f32)
    for t in range(4):
        out_ref[:, t * 32 : (t + 1) * 32, :] = scr_ref[t].reshape(16, 32, LANES).astype(bf16)
    keep = e_ref[...].astype(f32).astype(bf16)
    halves = [
        dot((iota((16, 32), 1) == 2 * iota((16, 32), 0) + s).astype(f32).astype(bf16), keep)
        for s in range(2)
    ]
    plane = jnp.concatenate(halves, axis=1)
    for j in range(16):
        out_ref[j, 128:136, :] = jnp.broadcast_to(plane[j : j + 1, :], (8, LANES)).astype(bf16)


def pack_cols_body(q_ref, k_ref, v_ref, g_ref, e_ref, out_ref):
    low = iota((16, LANES), 1) < 64
    for t, ref in enumerate((q_ref, k_ref, v_ref, g_ref)):
        for l in range(16):
            a = ref[0:16, l * LANES : (l + 1) * LANES].astype(f32)
            b = ref[16:32, l * LANES : (l + 1) * LANES].astype(f32)
            first = jnp.where(low, a, pltpu.roll(b, 64, 1))
            second = jnp.where(low, pltpu.roll(a, 64, 1), b)
            out_ref[2 * l, t * 16 : (t + 1) * 16, :] = first.astype(bf16)
            out_ref[2 * l + 1, t * 16 : (t + 1) * 16, :] = second.astype(bf16)
    keep = e_ref[...].astype(f32).astype(bf16)
    parts = [
        dot((iota((32, 64), 1) == 2 * iota((32, 64), 0) + pp).astype(f32).astype(bf16), keep, 1, 1)
        for pp in range(2)
    ]
    plane = jnp.concatenate(parts + [jnp.zeros((32, 64), f32)], axis=1)
    for i in range(32):
        out_ref[i, 64:72, :] = jnp.broadcast_to(plane[i : i + 1, :], (8, LANES)).astype(bf16)


def attend_body(rows, in_ref, out_ref, qx, gx, kx, kt, vx, dqt, dk, dv, st, da):
    peers = 16 if rows else 32
    items = 2 if rows else 1
    group = 256 if rows else 512
    turns = 4 if rows else 2
    turn = LANES // turns
    tensor_rows = 32 if rows else 16
    plane = in_ref[:, 4 * tensor_rows, :]
    lane = iota((group, LANES), 1)
    sub = iota((group, LANES), 0) % 16
    for item in range(items):
        parts = []
        for t in range(4):
            first = t * tensor_rows + item * 16
            parts.append(in_ref[:, first : first + 16, :].reshape(group, LANES).astype(f32))
        q4, k4, v4, g4 = parts
        spread = (iota((group, peers), 0) // 16 == iota((group, peers), 1)).astype(f32).astype(bf16)
        barred = 1.0 - dot(spread, plane)
        src, dst = iota((LANES, LANES), 0), iota((LANES, LANES), 1)
        if rows:
            here = lane // 4 == item * 16 + sub
            place = dst == CH * (src % 4)
        else:
            here = (lane % 16 == sub) & (lane < 64)
            place = dst == 64 * ((src // 16) % 2) + 32 * (src // 32)
        mark = jnp.where(here, barred, 0.0).astype(bf16)
        bias = dot(mark, place.astype(f32).astype(bf16)) * masked_score
        kt4 = k4.T
        for d in range(turns):
            span = slice(d * group, (d + 1) * group)

            def turned(x):
                return pltpu.roll(x, turn * d, 1) if d else x

            kx[item, span, 0:LANES] = turned(k4).astype(bf16)
            kx[item, span, LANES : 2 * LANES] = turned(bias).astype(bf16)
            vx[item, span, :] = turned(v4).astype(bf16)
            for a in range(BLOCKS):
                b = (a - d * turn // CH) % BLOCKS
                kt[item, a, :, span] = kt4[b * CH : (b + 1) * CH, :].astype(bf16)
        for a in range(BLOCKS):
            mine = lane // CH == a
            qa = jnp.where(mine, q4, 0.0).astype(bf16)
            ga = jnp.where(mine, g4, 0.0).astype(bf16)
            pick = (iota((QB, LANES), 1) == a * CH).astype(f32).astype(bf16)
            for part in range(group // QB):
                step = (item + part) * BLOCKS + a
                qx[step, :, 0:LANES] = qa[part * QB : (part + 1) * QB, :]
                qx[step, :, LANES : 2 * LANES] = pick
                gx[step] = ga[part * QB : (part + 1) * QB, :]
    dk[...] = jnp.zeros(dk.shape, f32)
    dv[...] = jnp.zeros(dv.shape, f32)
    chunks = [slice(c * KC, (c + 1) * KC) for c in range(KEYS // KC)]

    def one_step(step, carry):
        item = step // BLOCKS if rows else 0
        block = step % BLOCKS
        q = qx[step]
        g = gx[step]
        top = jnp.full((8, QB), -jnp.inf, f32)
        for c in chunks:
            s = dot(kx[item, c, :], q, 1, 1)
            st[c, :] = s
            top = jnp.maximum(top, jnp.max(s.reshape(KC // 8, 8, QB), axis=0))
            da[c, :] = dot(vx[item, c, :], g, 1, 1)
        top = jnp.max(top, axis=0, keepdims=True)
        total = jnp.zeros((8, QB), f32)
        inner = jnp.zeros((8, QB), f32)
        for c in chunks:
            e = jnp.exp2((st[c, :] - top) * EXP2_SCALE)
            st[c, :] = e
            total += jnp.sum(e.reshape(KC // 8, 8, QB), axis=0)
            inner += jnp.sum((e * da[c, :]).reshape(KC // 8, 8, QB), axis=0)
        inverse = 1.0 / jnp.sum(total, axis=0, keepdims=True)
        delta = jnp.sum(inner, axis=0, keepdims=True) * inverse
        dq = jnp.zeros((CH, QB), f32)
        for c in chunks:
            w = st[c, :] * inverse
            ds = (w * (da[c, :] - delta)).astype(bf16)
            dv[item, c, :] += dot(w.astype(bf16), g)
            dk[item, c, :] += dot(ds, q[:, 0:LANES])
            dq += dot(kt[item, block, :, c], ds)
        dqt[step] = dq
        return carry

    lax.fori_loop(0, 8, one_step, 0)

    for item in range(items):
        dq4 = [
            dqt[(item + part) * BLOCKS : (item + part + 1) * BLOCKS].reshape(LANES, QB).T
            for part in range(group // QB)
        ]
        sums = [jnp.concatenate(dq4, axis=0) * SCALE if len(dq4) > 1 else dq4[0] * SCALE]
        for acc, factor in ((dk, SCALE), (dv, 1.0)):
            total = acc[item, 0:group, :]
            for d in range(1, turns):
                total += pltpu.roll(acc[item, d * group : (d + 1) * group, :], LANES - turn * d, 1)
            sums.append(total * factor)
        for t in range(3):
            first = t * tensor_rows + item * 16
            out_ref[:, first : first + 16, :] = sums[t].reshape(peers, 16, LANES).astype(bf16)


def attend(rows, received):
    items = 2 if rows else 1
    peers = 16 if rows else 32
    scratch = [
        pltpu.VMEM((8, QB, 2 * LANES), bf16),
        pltpu.VMEM((8, QB, LANES), bf16),
        pltpu.VMEM((items, KEYS, 2 * LANES), bf16),
        pltpu.VMEM((items, BLOCKS, CH, KEYS), bf16),
        pltpu.VMEM((items, KEYS, LANES), bf16),
        pltpu.VMEM((8, CH, QB), f32),
        pltpu.VMEM((items, KEYS, LANES), f32),
        pltpu.VMEM((items, KEYS, LANES), f32),
        pltpu.VMEM((KEYS, QB), f32),
        pltpu.VMEM((KEYS, QB), f32),
    ]
    out = jax.ShapeDtypeStruct((peers, 96 if rows else 48, LANES), bf16)
    return call(functools.partial(attend_body, rows), out, scratch, received)


def unpack_rows_body(in_ref, out_ref, scr_ref):
    for t in range(3):
        scr_ref[t] = in_ref[:, t * 32 : (t + 1) * 32, :].reshape(512, LANES).astype(f32)
    for t in range(3):
        for l in range(16):
            out_ref[t, :, l * LANES : (l + 1) * LANES] = scr_ref[t, pl.ds(l, 32, stride=16), :]


def finish_body(rows_ref, in_ref, q_ref, k_ref, v_ref):
    low = iota((16, LANES), 1) < 64
    for t, ref in enumerate((q_ref, k_ref, v_ref)):
        for l in range(16):
            cols = slice(l * LANES, (l + 1) * LANES)
            a = in_ref[2 * l, t * 16 : (t + 1) * 16, :].astype(f32)
            b = in_ref[2 * l + 1, t * 16 : (t + 1) * 16, :].astype(f32)
            ref[0:16, cols] = rows_ref[t, 0:16, cols] + jnp.where(low, a, pltpu.roll(b, 64, 1))
            ref[16:32, cols] = rows_ref[t, 16:32, cols] + jnp.where(low, pltpu.roll(a, 64, 1), b)


def exchange(array, axis):
    return lax.all_to_all(array, axis, split_axis=0, concat_axis=0, tiled=True)


def pack_rows(*args):
    out = jax.ShapeDtypeStruct((16, 136, LANES), bf16)
    return call(pack_rows_body, out, [pltpu.VMEM((4, 512, LANES), f32)], *args)


def pack_cols(*args):
    return call(pack_cols_body, jax.ShapeDtypeStruct((32, 72, LANES), bf16), [], *args)


def unpack_rows(array):
    out = jax.ShapeDtypeStruct((3, 32, 2048), f32)
    return call(unpack_rows_body, out, [pltpu.VMEM((3, 512, LANES), f32)], array)


def finish(row_part, array):
    return call(finish_body, [jax.ShapeDtypeStruct((32, 2048), f32)] * 3, [], row_part, array)


def per_device(*args):
    row_in = exchange(pack_rows(*args), "prog")
    col_in = exchange(pack_cols(*args), "res")
    row_out = exchange(attend(True, row_in), "prog")
    col_out = exchange(attend(False, col_in), "res")
    return tuple(finish(unpack_rows(row_out), col_out))


def solution(mesh):
    return jax.shard_map(
        per_device,
        mesh=mesh,
        in_specs=(P("res", "prog"),) * 5,
        out_specs=(P("res", "prog"),) * 3,
        check_vma=False,
    )
```

time: 288 us -> 104 us (0.36)
  waiting for transfers between devices: 92.3 us -> 32.5 us
  starting transfers between devices: 89.1 us -> 37.2 us
  local copies, waits for them, and re-layouts: 49.3 us -> 4.35 us
  Pallas kernels: 0 us -> 28.6 us
  matrix products: 22.7 us -> 0 us
  loops' own time: 16.7 us -> 0 us
  other arithmetic: 15.4 us -> 0 us
    all_to_all x16 -> x4, waiting for transfers between devices: 92.3 us -> 32.5 us  [exchange(): return lax.all_to_all(array, axis, split_axis=0, concat_axis=0, tiled=True)]
    all_to_all x16 -> x4, starting transfers between devices: 89.1 us -> 37.2 us  [exchange(): return lax.all_to_all(array, axis, split_axis=0, concat_axis=0, tiled=True)]
    pallas_call x0 -> x6, Pallas kernels: none -> 28.6 us  [call(): pl.pallas_call(body, out_shape=outs, in_specs=[pl.BlockSpec(memory_space=...]
    dot_general x48 -> x0, matrix products: 22.7 us -> none  [the longest x8 5.9 us: block_grads(): jnp.dot(cot_block, value_rows.T, preferred_element_type=jnp.float32)]
    unnamed x54 -> x20, local copies, waits for them, and re-layouts: 21.4 us -> 4.35 us
    another operation x6 -> x0, loops' own time: 16.7 us -> none  [the longest x4 16.3 us: item_body(): lax.scan(block_step, zero_sums, offsets)]
    convert_element_type x10 -> x0, local copies, waits for them, and re-layouts: 7.29 us -> none  [the longest x3 4.06 us: per_device(): col_grads[slot].astype(jnp.float32)]
    while x18 -> x0, local copies, waits for them, and re-layouts: 5.67 us -> none  [the longest x6 5.17 us: pass_grads(): return lax.fori_loop(0, item_count, item_body, (empty, empty, empty))]
  transfers between devices with their start and end apart: 16 -> 4, of which waited for: 14 -> 3; matrix products, arithmetic and copies ran while one was open for 28% -> 0% of each run, Pallas kernels for 0% -> 25%
where the time goes in v1:
time: 104 us; the launch traced here: 103 us
  starting transfers between devices  37.2 us (36%)
  waiting for transfers between devices  32.5 us (31%)
  Pallas kernels  28.6 us (28%)
  local copies, waits for them, and re-layouts  4.35 us (4%)
    all_to_all x4, starting transfers between devices, exchange(): return lax.all_to_all(array, axis, split_axis=0, concat_axis=0, tiled=True)  37.2 us
    all_to_all x4, waiting for transfers between devices, exchange(): return lax.all_to_all(array, axis, split_axis=0, concat_axis=0, tiled=True)  32.5 us
    pallas_call x6, Pallas kernels, call(): pl.pallas_call(body, out_shape=outs, in_specs=[pl.BlockSpec(memory_space=...  28.6 us
    unnamed x20, local copies, waits for them, and re-layouts  4.35 us
  transfers between devices with their start and end apart: 4, of which 3 were waited for; matrix products, arithmetic and copies ran while one was open for 0% of the time, Pallas kernels for 25%

profile of v1, /device:TPU:1, one launch (start us, length us, event | category | flops | bytes accessed | tf_op | source)
XLA Modules:
  0.0 103.4 jit_solution(4102248608271599840)
XLA Ops:
  0.6 0.0 copy-start
  0.6 0.9 copy-done
  1.5 0.0 copy-start.2
  1.5 0.9 copy-done.2
  2.4 0.0 copy-start.4
  2.4 0.9 copy-done.4
  3.3 0.0 copy-start.6
  3.3 0.9 copy-done.6
  4.3 0.0 copy-start.8
  4.3 0.7 copy-done.8
  5.0 1.4 %shard_map.76 = bf16[16,136,128]{2,1,0:T(8,128)(2,1)} custom-call(bf16[32,2048]{1,0:T(8,128)(2,1)S(1)} %copy-done, bf16[32,2048]{1,0:T(8,128)(2,1)S(1)} %copy-done.2, bf16[32,2048]{1,0:T(8,128)(2,1)S(1)} %copy-done.4, bf16[32,2048]{1,0:T(8,128)(2,1)S(1)} %copy-done.6, s32[32,64]{1,0:T(8,128)S(1)} %copy-done.8), custom_call_target="tpu_custom_call" | custom-call | tf_op jit(solution)/shard_map/pallas_call | solution.py:35
  6.4 0.0 copy-start.1
  6.4 0.0 copy-start.3
  6.4 0.0 copy-start.9
  6.4 12.1 %all-to-all-start = ((bf16[16,136,128]{2,1,0:T(8,128)(2,1)}), bf16[16,136,128]{2,1,0:T(8,128)(2,1)S(1)}, u32[]{:S(2)}, u32[]{:S(2)}) async-start(bf16[16,136,128]{2,1,0:T(8,128)(2,1)} %shard_map.76), calls=%async_computation | async-start | bytes 1114112 | tf_op jit(solution)/shard_map/all_to_all | solution.py:224
  18.5 0.0 copy-done.1
  18.5 0.0 copy-done.3
  18.5 0.0 copy-done.5
  18.5 0.0 copy-done.7
  18.5 0.0 copy-done.9
  18.6 1.1 %shard_map.79 = bf16[32,72,128]{2,1,0:T(8,128)(2,1)} custom-call(bf16[32,2048]{1,0:T(8,128)(2,1)S(1)} %copy-done.1, bf16[32,2048]{1,0:T(8,128)(2,1)S(1)} %copy-done.3, bf16[32,2048]{1,0:T(8,128)(2,1)S(1)} %copy-done.5, bf16[32,2048]{1,0:T(8,128)(2,1)S(1)} %copy-done.7, s32[32,64]{1,0:T(8,128)S(1)} %copy-done.9), custom_call_target="tpu_custom_call" | custom-call | tf_op jit(solution)/shard_map/pallas_call | solution.py:35
  19.6 11.5 %all-to-all-done.in_ref = bf16[16,136,128]{2,1,0:T(8,128)(2,1)S(1)} async-done(((bf16[16,136,128]{2,1,0:T(8,128)(2,1)}), bf16[16,136,128]{2,1,0:T(8,128)(2,1)S(1)}, u32[]{:S(2)}, u32[]{:S(2)}) %all-to-all-start) | async-done | bytes 557088 | tf_op jit(solution)/shard_map/all_to_all | solution.py:224
  31.2 13.1 %all-to-all-start.2 = ((bf16[32,72,128]{2,1,0:T(8,128)(2,1)}), bf16[32,72,128]{2,1,0:T(8,128)(2,1)S(1)}, u32[]{:S(2)}, u32[]{:S(2)}) async-start(bf16[32,72,128]{2,1,0:T(8,128)(2,1)} %shard_map.79), calls=%async_computation.2 | async-start | bytes 1179648 | tf_op jit(solution)/shard_map/all_to_all | solution.py:224
  44.2 12.7 %shard_map.77 = bf16[16,96,128]{2,1,0:T(8,128)(2,1)} custom-call(bf16[16,136,128]{2,1,0:T(8,128)(2,1)S(1)} %all-to-all-done.in_ref), custom_call_target="tpu_custom_call" | custom-call | tf_op jit(solution)/shard_map/pallas_call | solution.py:35
  56.9 5.6 %all-to-all-done.2.in_ref = bf16[32,72,128]{2,1,0:T(8,128)(2,1)S(1)} async-done(((bf16[32,72,128]{2,1,0:T(8,128)(2,1)}), bf16[32,72,128]{2,1,0:T(8,128)(2,1)S(1)}, u32[]{:S(2)}, u32[]{:S(2)}) %all-to-all-start.2) | async-done | bytes 589856 | tf_op jit(solution)/shard_map/all_to_all | solution.py:224
  62.5 7.0 %all-to-all-start.1 = ((bf16[16,96,128]{2,1,0:T(8,128)(2,1)}), bf16[16,96,128]{2,1,0:T(8,128)(2,1)S(1)}, u32[]{:S(2)}, u32[]{:S(2)}) async-start(bf16[16,96,128]{2,1,0:T(8,128)(2,1)} %shard_map.77), calls=%async_computation.1 | async-start | bytes 786432 | tf_op jit(solution)/shard_map/all_to_all | solution.py:224
  69.5 12.2 %shard_map.80 = bf16[32,48,128]{2,1,0:T(8,128)(2,1)} custom-call(bf16[32,72,128]{2,1,0:T(8,128)(2,1)S(1)} %all-to-all-done.2.in_ref), custom_call_target="tpu_custom_call" | custom-call | tf_op jit(solution)/shard_map/pallas_call | solution.py:35
  81.6 0.0 all-to-all-done.1.in_ref
  81.7 5.0 %all-to-all-start.3 = ((bf16[32,48,128]{2,1,0:T(8,128)(2,1)}), bf16[32,48,128]{2,1,0:T(8,128)(2,1)S(1)}, u32[]{:S(2)}, u32[]{:S(2)}) async-start(bf16[32,48,128]{2,1,0:T(8,128)(2,1)} %shard_map.80), calls=%async_computation.3 | async-start | bytes 786432 | tf_op jit(solution)/shard_map/all_to_all | solution.py:224
  86.7 0.3 shard_map.78.rows_ref
  87.0 15.4 %all-to-all-done.3.in_ref = bf16[32,48,128]{2,1,0:T(8,128)(2,1)S(1)} async-done(((bf16[32,48,128]{2,1,0:T(8,128)(2,1)}), bf16[32,48,128]{2,1,0:T(8,128)(2,1)S(1)}, u32[]{:S(2)}, u32[]{:S(2)}) %all-to-all-start.3) | async-done | bytes 393248 | tf_op jit(solution)/shard_map/all_to_all | solution.py:224
  102.4 1.0 shard_map.81
  (2 shorter events, 0.0 us)
Async XLA Ops:
  0.6 0.9 copy-start
  1.5 0.9 copy-start.2
  2.4 0.9 copy-start.4
  3.3 0.9 copy-start.6
  4.3 0.7 copy-start.8
  6.4 12.1 %copy-start.1 = (bf16[32,2048]{1,0:T(8,128)(2,1)S(1)}, bf16[32,2048]{1,0:T(8,128)(2,1)}, u32[]{:S(2)}) copy-start(bf16[32,2048]{1,0:T(8,128)(2,1)} %q_ref.3) | copy-start | bytes 393220
  6.4 12.2 %copy-start.3 = (bf16[32,2048]{1,0:T(8,128)(2,1)S(1)}, bf16[32,2048]{1,0:T(8,128)(2,1)}, u32[]{:S(2)}) copy-start(bf16[32,2048]{1,0:T(8,128)(2,1)} %k_ref.3) | copy-start | bytes 393220
  6.4 12.2 %copy-start.5 = (bf16[32,2048]{1,0:T(8,128)(2,1)S(1)}, bf16[32,2048]{1,0:T(8,128)(2,1)}, u32[]{:S(2)}) copy-start(bf16[32,2048]{1,0:T(8,128)(2,1)} %v_ref.3) | copy-start | bytes 393220
  6.4 12.2 %copy-start.7 = (bf16[32,2048]{1,0:T(8,128)(2,1)S(1)}, bf16[32,2048]{1,0:T(8,128)(2,1)}, u32[]{:S(2)}) copy-start(bf16[32,2048]{1,0:T(8,128)(2,1)} %g_ref.3) | copy-start | bytes 393220
  6.4 12.2 %copy-start.9 = (s32[32,64]{1,0:T(8,128)S(1)}, s32[32,64]{1,0:T(8,128)}, u32[]{:S(2)}) copy-start(s32[32,64]{1,0:T(8,128)} %e_ref.3) | copy-start | bytes 24580
  6.4 24.8 %all-to-all-start = ((bf16[16,136,128]{2,1,0:T(8,128)(2,1)}), bf16[16,136,128]{2,1,0:T(8,128)(2,1)S(1)}, u32[]{:S(2)}, u32[]{:S(2)}) async-start(bf16[16,136,128]{2,1,0:T(8,128)(2,1)} %shard_map.76), calls=%async_computation | async-start | bytes 1114112 | tf_op jit(solution)/shard_map/all_to_all | solution.py:224
  31.2 31.3 %all-to-all-start.2 = ((bf16[32,72,128]{2,1,0:T(8,128)(2,1)}), bf16[32,72,128]{2,1,0:T(8,128)(2,1)S(1)}, u32[]{:S(2)}, u32[]{:S(2)}) async-start(bf16[32,72,128]{2,1,0:T(8,128)(2,1)} %shard_map.79), calls=%async_computation.2 | async-start | bytes 1179648 | tf_op jit(solution)/shard_map/all_to_all | solution.py:224
  62.5 19.2 %all-to-all-start.1 = ((bf16[16,96,128]{2,1,0:T(8,128)(2,1)}), bf16[16,96,128]{2,1,0:T(8,128)(2,1)S(1)}, u32[]{:S(2)}, u32[]{:S(2)}) async-start(bf16[16,96,128]{2,1,0:T(8,128)(2,1)} %shard_map.77), calls=%async_computation.1 | async-start | bytes 786432 | tf_op jit(solution)/shard_map/all_to_all | solution.py:224
  81.7 20.7 %all-to-all-start.3 = ((bf16[32,48,128]{2,1,0:T(8,128)(2,1)}), bf16[32,48,128]{2,1,0:T(8,128)(2,1)S(1)}, u32[]{:S(2)}, u32[]{:S(2)}) async-start(bf16[32,48,128]{2,1,0:T(8,128)(2,1)} %shard_map.80), calls=%async_computation.3 | async-start | bytes 786432 | tf_op jit(solution)/shard_map/all_to_all | solution.py:224
